TPU v7x, 32 devices: a whole 2x2x4 slice. The times are simulated.
32 devices in a mesh: gz: 16 (over z, y, core), ta: 2 (over x).
Axes of the slice: x: 2, y: 2, z: 4, core: 2. Of those that a mesh axis runs over, the one named last changes fastest.
Arguments:
- outputs_fwd: bfloat16 [4, 32, 64, 1280], P('ta', 'gz'), may hold values from -6 to 6
- cotangent: bfloat16 [4, 32, 64, 1280], P('ta', 'gz'), may hold values from -6 to 6
- spatial_weight: bfloat16 [3, 64, 288], replicated, may hold values from -0.21875 to 0.21875
- hidden_bias: float32 [64], replicated, may hold values from -1 to 1
- temporal_weight: bfloat16 [3, 32, 64], replicated, may hold values from -0.4375 to 0.4375
Outputs:
- rebuilt: bfloat16 [4, 32, 32, 1280], P('ta', 'gz')
- grad_in: bfloat16 [4, 32, 32, 1280], P('ta', 'gz')
- grad_spatial: float32 [3, 64, 288], replicated
- grad_bias: float32 [64], replicated
- grad_temporal: float32 [3, 32, 64], replicated
All inputs are finite; a program needn't handle non-finite values.
Results may differ from a plain program's by a relative error of at most 0.0075.
Values may be sent and summed in bfloat16 or wider, within the bound.
A program may use at most 64 MiB of HBM per device.

v0:
```python
import math
import jax
import jax.numpy as jnp
from jax import lax
from jax.sharding import PartitionSpec as P

ROWS = 8
COLS = 160


def with_halo(cells, sides, width, closed):
    for axis, dim in sides:
        count = lax.axis_size(axis)
        ends = count if closed else count - 1
        head = lax.slice_in_dim(cells, 0, width, axis=dim)
        tail = lax.slice_in_dim(cells, cells.shape[dim] - width, cells.shape[dim], axis=dim)
        cells = jnp.concatenate(
            [
                lax.ppermute(tail, axis, [(i, (i + 1) % count) for i in range(ends)]),
                cells,
                lax.ppermute(head, axis, [((i + 1) % count, i) for i in range(ends)]),
            ],
            axis=dim,
        )
    return cells


def unfold(field):
    leading = field.shape[:-1]
    planar = field.reshape(leading + (ROWS, COLS))
    padded = jnp.pad(planar, [(0, 0)] * len(leading) + [(1, 1), (1, 1)])
    windows = [
        padded[..., row_off : row_off + ROWS, col_off : col_off + COLS]
        for row_off in range(3)
        for col_off in range(3)
    ]
    stacked = jnp.stack(windows, axis=-4)
    return stacked.reshape(leading[:-1] + (9 * leading[-1], ROWS * COLS))


def spatial(columns, spatial_weight, plane_count):
    total = jnp.einsum(
        "oi,fzir->fzor",
        spatial_weight[0],
        columns[:, 0:plane_count],
        preferred_element_type=jnp.float32,
    )
    total = total + jnp.einsum(
        "oi,fzir->fzor",
        spatial_weight[1],
        columns[:, 1 : plane_count + 1],
        preferred_element_type=jnp.float32,
    )
    total = total + jnp.einsum(
        "oi,fzir->fzor",
        spatial_weight[2],
        columns[:, 2 : plane_count + 2],
        preferred_element_type=jnp.float32,
    )
    return total


def temporal_back(temporal_weight, grad_around, frame_count):
    through = jnp.einsum(
        "oi,fzor->fzir",
        temporal_weight[0],
        grad_around[2 : frame_count + 2],
        preferred_element_type=jnp.float32,
    )
    through = through + jnp.einsum(
        "oi,fzor->fzir",
        temporal_weight[1],
        grad_around[1 : frame_count + 1],
        preferred_element_type=jnp.float32,
    )
    through = through + jnp.einsum(
        "oi,fzor->fzir",
        temporal_weight[2],
        grad_around[0:frame_count],
        preferred_element_type=jnp.float32,
    )
    return through


def hidden_gradient(through, hidden_in):
    sigmoid_val = jax.nn.sigmoid(hidden_in)
    return (through * sigmoid_val * (1.0 + hidden_in * (1.0 - sigmoid_val))).astype(jnp.bfloat16)


def shards(outputs_fwd, cotangent, spatial_weight, hidden_bias, temporal_weight):
    half = spatial_weight.shape[2] // 9
    hidden_count = spatial_weight.shape[1]
    front_half = outputs_fwd[:, :, :half]
    back_half = outputs_fwd[:, :, half:]
    grad_front = cotangent[:, :, :half]
    grad_back = cotangent[:, :, half:]
    frame_count = front_half.shape[0]
    plane_count = front_half.shape[1]
    bias_row = hidden_bias[None, None, :, None]
    depth_rim = 1
    padded_wide = with_halo(front_half, (("gz", 1),), depth_rim, False)
    columns = unfold(padded_wide)
    hidden_in = spatial(columns, spatial_weight, plane_count) + bias_row
    active = jax.nn.silu(hidden_in).astype(jnp.bfloat16)
    beside_all = with_halo(active, (("ta", 0),), 1, True)
    mapped = jnp.einsum(
        "oi,fzir->fzor",
        temporal_weight[0],
        beside_all[0:frame_count],
        preferred_element_type=jnp.float32,
    )
    mapped = mapped + jnp.einsum(
        "oi,fzir->fzor",
        temporal_weight[1],
        beside_all[1 : frame_count + 1],
        preferred_element_type=jnp.float32,
    )
    mapped = mapped + jnp.einsum(
        "oi,fzir->fzor",
        temporal_weight[2],
        beside_all[2 : frame_count + 2],
        preferred_element_type=jnp.float32,
    )
    rebuilt = (back_half.astype(jnp.float32) - mapped).astype(jnp.bfloat16)
    grad_around = with_halo(grad_back, (("ta", 0),), 1, True)
    through = temporal_back(temporal_weight, grad_around, frame_count)
    temporal_grad = jnp.stack(
        [
            jnp.einsum(
                "fzor,fzir->oi",
                grad_back,
                beside_all[offset : offset + frame_count],
                preferred_element_type=jnp.float32,
            )
            for offset in range(3)
        ]
    )
    hidden_grad = hidden_gradient(through, hidden_in)
    spatial_grad = jnp.stack(
        [
            jnp.einsum(
                "fzor,fzir->oi",
                hidden_grad,
                columns[:, depth : depth + plane_count],
                preferred_element_type=jnp.float32,
            )
            for depth in range(3)
        ]
    )
    bias_grad = jnp.einsum("fzor->o", hidden_grad.astype(jnp.float32))
    grad_planes = with_halo(hidden_grad, (("gz", 1),), 1, False)
    flipped = (
        spatial_weight.reshape((3, hidden_count, 9, half))[:, :, ::-1]
        .transpose((0, 3, 2, 1))
        .reshape((3, half, 9 * hidden_count))
    )

    def adjoint_frame(frame_planes):
        grad_columns = unfold(frame_planes)
        total = jnp.einsum(
            "ci,zir->zcr",
            flipped[0],
            grad_columns[2 : plane_count + 2],
            preferred_element_type=jnp.float32,
        )
        total = total + jnp.einsum(
            "ci,zir->zcr",
            flipped[1],
            grad_columns[1 : plane_count + 1],
            preferred_element_type=jnp.float32,
        )
        total = total + jnp.einsum(
            "ci,zir->zcr",
            flipped[2],
            grad_columns[0:plane_count],
            preferred_element_type=jnp.float32,
        )
        return total

    input_grad = lax.map(adjoint_frame, grad_planes)
    grad_in = (grad_front.astype(jnp.float32) + input_grad).astype(jnp.bfloat16)
    totals = lax.psum((spatial_grad, bias_grad, temporal_grad), ("gz", "ta"))
    factor = 1.0 / math.sqrt(
        frame_count * lax.axis_size("ta") * plane_count * lax.axis_size("gz") * ROWS * COLS
    )
    return (rebuilt, grad_in, totals[0] * factor, totals[1] * factor, totals[2] * factor)


def solution(mesh):
    placed = (P("ta", "gz", None, None), P("ta", "gz", None, None), P(), P(), P())
    return jax.shard_map(
        shards,
        mesh=mesh,
        in_specs=placed,
        out_specs=(P("ta", "gz", None, None), P("ta", "gz", None, None), P(), P(), P()),
        check_vma=False,
    )
```

profile of v0, /device:TPU:0, one launch (start us, length us, event | category | flops | bytes accessed | tf_op | source)
XLA Modules:
  0.0 338.4 jit_solution(7033846811327867473)
XLA Ops:
  8.3 2.4 collective-permute-start
  12.1 1.7 fusion.123
  13.7 2.3 collective-permute-start.4
  16.1 1.7 slice.236
  31.7 1.7 fusion.66
  36.2 15.8 %reshape.46 = bf16[2,4,288,1280]{3,2,1,0:T(8,128)(2,1)} reshape(bf16[2,4,9,32,8,160]{5,4,3,2,1,0:T(8,128)(2,1)} %fusion.70) | data formatting | bytes 11796480 | tf_op jit(solution)/shard_map/reshape | solution.py:38
  52.0 2.7 fusion.40
  54.7 2.6 convolution_add_fusion.4
  59.9 1.8 convert_reduce_fusion
  67.8 4.3 %collective-permute-start.6 = (bf16[2,1,64,1280]{3,2,1,0:T(8,128)(2,1)S(1)}, bf16[2,1,64,1280]{3,2,1,0:T(8,128)(2,1)S(1)}, u32[]{:S(2)}, u32[]{:S(2)}) collective-permute-start(bf16[2,1,64,1280]{3,2,1,0:T(8,128)(2,1)S(1)} %get-tuple-element.72), channel_id=1, source_target_pairs={{0,2},{2,4},{4,6},{6,8},{8,10},{10,12},{12,14},{14,16},{16,18},{18... | collective-permute-start | bytes 983048 | tf_op jit(solution)/shard_map/ppermute | solution.py:19
  75.8 124.2 %all-reduce.5.cloned.1.call-done = f32[3,64,288]{2,1,0:T(8,128)} async-done(((f32[3,64,288]{2,1,0:T(8,128)}), f32[3,64,288]{2,1,0:T(8,128)}) %all-reduce.5.cloned.1.call-update) | async-done | bytes 221200 | tf_op jit(solution)/shard_map/psum | solution.py:182
  200.0 1.7 broadcast_multiply_fusion
  202.9 77.5 %while.12 = (s32[]{:T(128)}, f32[2,2,32,1280]{3,2,1,0:T(8,128)}, bf16[2,4,64,1280]{3,2,1,0:T(8,128)(2,1)}, bf16[3,32,576]{2,1,0:T(8,128)(2,1)S(1)}, s32[]{:T(128)}) while((s32[]{:T(128)}, f32[2,2,32,1280]{3,2,1,0:T(8,128)}, bf16[2,4,64,1280]{3,2,1,0:T(8,128)(2,1)}, bf16[3,32,576]{2,1,0:T(8,128)(2,1)S(1)}, s32[]{:T(128)}) %tuple.40), condition=%wide.region_1.2_spmd, body=%wide.region_0.1_spmd.sunk | while | flops 283279360 | bytes 69722216 | solution.py:180
  210.7 5.4 %fusion.165 = (bf16[2,9,64,8,160]{4,3,2,1,0:T(8,128)(2,1)}, bf16[2,9,64,8,160]{4,3,2,1,0:T(8,128)(2,1)}, bf16[2,9,64,8,160]{4,3,2,1,0:T(8,128)(2,1)}) fusion(bf16[4,9,64,8,160]{4,3,2,1,0:T(8,128)(2,1)S(1)} %fusion.164), kind=kLoop, calls=%fused_computation.155.clone.1 | loop fusion | bytes 17694720 | tf_op jit(solution)/shard_map/while/body/eval_jaxpr/slice | solution.py:175
  216.1 7.4 %slice.457 = bf16[2,576,1280]{2,1,0:T(8,128)(2,1)S(1)} reshape(bf16[2,9,64,8,160]{4,3,2,1,0:T(8,128)(2,1)} %get-tuple-element.112) | data formatting | bytes 5898240 | tf_op jit(solution)/shard_map/while/body/eval_jaxpr/slice | solution.py:163
  224.1 7.4 %slice.458 = bf16[2,576,1280]{2,1,0:T(8,128)(2,1)S(1)} reshape(bf16[2,9,64,8,160]{4,3,2,1,0:T(8,128)(2,1)} %get-tuple-element.113) | data formatting | bytes 5898240 | tf_op jit(solution)/shard_map/while/body/eval_jaxpr/slice | solution.py:169
  232.9 7.4 %slice.459 = bf16[2,576,1280]{2,1,0:T(8,128)(2,1)S(1)} reshape(bf16[2,9,64,8,160]{4,3,2,1,0:T(8,128)(2,1)} %get-tuple-element.114) | data formatting | bytes 5898240 | tf_op jit(solution)/shard_map/while/body/eval_jaxpr/slice | solution.py:175
  249.5 5.4 %fusion.165 = (bf16[2,9,64,8,160]{4,3,2,1,0:T(8,128)(2,1)}, bf16[2,9,64,8,160]{4,3,2,1,0:T(8,128)(2,1)}, bf16[2,9,64,8,160]{4,3,2,1,0:T(8,128)(2,1)}) fusion(bf16[4,9,64,8,160]{4,3,2,1,0:T(8,128)(2,1)S(1)} %fusion.164), kind=kLoop, calls=%fused_computation.155.clone.1 | loop fusion | bytes 17694720 | tf_op jit(solution)/shard_map/while/body/eval_jaxpr/slice | solution.py:175
  254.9 7.4 %slice.457 = bf16[2,576,1280]{2,1,0:T(8,128)(2,1)S(1)} reshape(bf16[2,9,64,8,160]{4,3,2,1,0:T(8,128)(2,1)} %get-tuple-element.112) | data formatting | bytes 5898240 | tf_op jit(solution)/shard_map/while/body/eval_jaxpr/slice | solution.py:163
  262.9 7.4 %slice.458 = bf16[2,576,1280]{2,1,0:T(8,128)(2,1)S(1)} reshape(bf16[2,9,64,8,160]{4,3,2,1,0:T(8,128)(2,1)} %get-tuple-element.113) | data formatting | bytes 5898240 | tf_op jit(solution)/shard_map/while/body/eval_jaxpr/slice | solution.py:169
  271.7 7.4 %slice.459 = bf16[2,576,1280]{2,1,0:T(8,128)(2,1)S(1)} reshape(bf16[2,9,64,8,160]{4,3,2,1,0:T(8,128)(2,1)} %get-tuple-element.114) | data formatting | bytes 5898240 | tf_op jit(solution)/shard_map/while/body/eval_jaxpr/slice | solution.py:175
  280.5 2.1 add_convert_fusion
  285.5 41.7 %all-reduce.2 = (f32[64]{0:T(128)S(1)}, f32[3,32,64]{2,1,0:T(8,128)S(1)}) all-reduce(f32[64]{0:T(128)S(1)} %get-tuple-element.82, f32[3,32,64]{2,1,0:T(8,128)S(1)} %pad_maximum_fusion.3), channel_id=1, replica_groups=mesh['gz'=16,'ta'=2] {'gz','ta'}, use_global_device_ids=true, to_apply=%region_4.5 | all-reduce | flops 6208 | bytes 49664 | tf_op jit(solution)/shard_map/psum | solution.py:182
  329.6 1.9 fusion.45
  (110 shorter events, 59.7 us)
Async XLA Ops:
  7.2 13.6 %slice-start = ((bf16[2,2,64,1280]{3,2,1,0:T(8,128)(2,1)}), bf16[2,2,32,1280]{3,2,1,0:T(8,128)(2,1)S(1)}, s32[]{:S(2)}) async-start(bf16[2,2,64,1280]{3,2,1,0:T(8,128)(2,1)} %param.7), calls=%async_computation.1 | async-start | bytes 655360 | tf_op jit(solution)/shard_map/slice | solution.py:93
  7.2 12.1 %copy-start.4 = (bf16[2,2,64,1280]{3,2,1,0:T(8,128)(2,1)S(1)}, bf16[2,2,64,1280]{3,2,1,0:T(8,128)(2,1)}, u32[]{:S(2)}) copy-start(bf16[2,2,64,1280]{3,2,1,0:T(8,128)(2,1)} %param.8) | copy-start | bytes 1966084
  7.2 12.1 %copy-start.11 = (bf16[3,32,64]{2,1,0:T(8,128)(2,1)S(1)}, bf16[3,32,64]{2,1,0:T(8,128)(2,1)}, u32[]{:S(2)}) copy-start(bf16[3,32,64]{2,1,0:T(8,128)(2,1)} %param.11) | copy-start | bytes 36868
  7.2 192.8 %all-reduce.5.cloned.1.call-start = ((), (), s32[]{:S(2)}) async-start(), calls=%async_computation | async-start | bytes 589824 | tf_op jit(solution)/shard_map/psum | solution.py:182
  8.3 12.4 %collective-permute-start = (bf16[2,1,32,1280]{3,2,1,0:T(8,128)(2,1)S(1)}, bf16[2,1,32,1280]{3,2,1,0:T(8,128)(2,1)S(1)}, u32[]{:S(2)}, u32[]{:S(2)}) collective-permute-start(bf16[2,1,32,1280]{3,2,1,0:T(8,128)(2,1)S(1)} %get-tuple-element.78), channel_id=1, source_target_pairs={{0,2},{2,4},{4,6},{6,8},{8,10},{10,12},{12,14},{14,16},{16,18},{18... | collective-permute-start | bytes 491528 | tf_op jit(solution)/shard_map/ppermute | solution.py:19
  10.8 10.0 %collective-permute-start.1 = (bf16[2,1,32,1280]{3,2,1,0:T(8,128)(2,1)S(1)}, bf16[2,1,32,1280]{3,2,1,0:T(8,128)(2,1)S(1)}, u32[]{:S(2)}, u32[]{:S(2)}) collective-permute-start(bf16[2,1,32,1280]{3,2,1,0:T(8,128)(2,1)S(1)} %get-tuple-element.79), channel_id=1, source_target_pairs={{2,0},{4,2},{6,4},{8,6},{10,8},{12,10},{14,12},{16,14},{18,16},{20... | collective-permute-start | bytes 491528 | tf_op jit(solution)/shard_map/ppermute | solution.py:21
  13.7 46.1 %collective-permute-start.4 = (bf16[1,2,32,1280]{3,2,1,0:T(8,128)(2,1)}, bf16[1,2,32,1280]{3,2,1,0:T(8,128)(2,1)}, u32[]{:S(2)}, u32[]{:S(2)}) collective-permute-start(bf16[1,2,32,1280]{3,2,1,0:T(8,128)(2,1)} %get-tuple-element.74), channel_id=1, source_target_pairs={{1,0},{0,1},{3,2},{2,3},{5,4},{4,5},{7,6},{6,7},{9,8},{8,9},{11,10... | collective-permute-start | bytes 491528 | tf_op jit(solution)/shard_map/ppermute | solution.py:21
  16.1 42.3 %collective-permute-start.5 = (bf16[1,2,32,1280]{3,2,1,0:T(8,128)(2,1)S(1)}, bf16[1,2,32,1280]{3,2,1,0:T(8,128)(2,1)}, u32[]{:S(2)}, u32[]{:S(2)}) collective-permute-start(bf16[1,2,32,1280]{3,2,1,0:T(8,128)(2,1)S(1)} %get-tuple-element.75), channel_id=1, source_target_pairs={{0,1},{1,0},{2,3},{3,2},{4,5},{5,4},{6,7},{7,6},{8,9},{9,8},{10,11... | collective-permute-start | bytes 491528 | tf_op jit(solution)/shard_map/ppermute | solution.py:19
  36.2 15.8 %copy-start.10 = (bf16[3,64,288]{2,1,0:T(8,128)(2,1)S(1)}, bf16[3,64,288]{2,1,0:T(8,128)(2,1)}, u32[]{:S(2)}) copy-start(bf16[3,64,288]{2,1,0:T(8,128)(2,1)} %param.9) | copy-start | bytes 331780
  52.0 5.4 %copy-start.1 = (bf16[2,4,288,1280]{3,2,1,0:T(8,128)(2,1)S(1)}, bf16[2,4,288,1280]{3,2,1,0:T(8,128)(2,1)}, u32[]{:S(2)}) copy-start(bf16[2,4,288,1280]{3,2,1,0:T(8,128)(2,1)} %reshape.46) | copy-start | bytes 17694724
  54.7 2.7 copy-start.12
  57.4 1.0 copy-start.8
  57.4 2.5 copy-start.9
  58.3 17.2 %copy-start.2 = (bf16[2,2,64,1280]{3,2,1,0:T(8,128)(2,1)}, bf16[2,2,64,1280]{3,2,1,0:T(8,128)(2,1)S(1)}, u32[]{:S(2)}) copy-start(bf16[2,2,64,1280]{3,2,1,0:T(8,128)(2,1)S(1)} %get-tuple-element.80) | copy-start | bytes 1966084
  65.0 10.5 %copy-start.5 = (bf16[2,2,64,1280]{3,2,1,0:T(8,128)(2,1)S(1)}, bf16[2,2,64,1280]{3,2,1,0:T(8,128)(2,1)}, u32[]{:S(2)}) copy-start(bf16[2,2,64,1280]{3,2,1,0:T(8,128)(2,1)} %param.8) | copy-start | bytes 1966084
  67.8 133.9 %collective-permute-start.6 = (bf16[2,1,64,1280]{3,2,1,0:T(8,128)(2,1)S(1)}, bf16[2,1,64,1280]{3,2,1,0:T(8,128)(2,1)S(1)}, u32[]{:S(2)}, u32[]{:S(2)}) collective-permute-start(bf16[2,1,64,1280]{3,2,1,0:T(8,128)(2,1)S(1)} %get-tuple-element.72), channel_id=1, source_target_pairs={{0,2},{2,4},{4,6},{6,8},{8,10},{10,12},{12,14},{14,16},{16,18},{18... | collective-permute-start | bytes 983048 | tf_op jit(solution)/shard_map/ppermute | solution.py:19
  72.1 129.6 %collective-permute-start.7 = (bf16[2,1,64,1280]{3,2,1,0:T(8,128)(2,1)S(1)}, bf16[2,1,64,1280]{3,2,1,0:T(8,128)(2,1)S(1)}, u32[]{:S(2)}, u32[]{:S(2)}) collective-permute-start(bf16[2,1,64,1280]{3,2,1,0:T(8,128)(2,1)S(1)} %get-tuple-element.73), channel_id=1, source_target_pairs={{2,0},{4,2},{6,4},{8,6},{10,8},{12,10},{14,12},{16,14},{18,16},{20... | collective-permute-start | bytes 983048 | tf_op jit(solution)/shard_map/ppermute | solution.py:21
  73.4 209.2 %collective-permute-start.2 = (bf16[1,2,64,1280]{3,2,1,0:T(8,128)(2,1)}, bf16[1,2,64,1280]{3,2,1,0:T(8,128)(2,1)}, u32[]{:S(2)}, u32[]{:S(2)}) collective-permute-start(bf16[1,2,64,1280]{3,2,1,0:T(8,128)(2,1)} %get-tuple-element.76), channel_id=1, source_target_pairs={{0,1},{1,0},{2,3},{3,2},{4,5},{5,4},{6,7},{7,6},{8,9},{9,8},{10,11... | collective-permute-start | bytes 983048 | tf_op jit(solution)/shard_map/ppermute | solution.py:19
  75.0 209.1 %collective-permute-start.3 = (bf16[1,2,64,1280]{3,2,1,0:T(8,128)(2,1)}, bf16[1,2,64,1280]{3,2,1,0:T(8,128)(2,1)}, u32[]{:S(2)}, u32[]{:S(2)}) collective-permute-start(bf16[1,2,64,1280]{3,2,1,0:T(8,128)(2,1)} %get-tuple-element.77), channel_id=1, source_target_pairs={{1,0},{0,1},{3,2},{2,3},{5,4},{4,5},{7,6},{6,7},{9,8},{8,9},{11,10... | collective-permute-start | bytes 983048 | tf_op jit(solution)/shard_map/ppermute | solution.py:21
  232.9 7.5 %copy-start = (f32[2,1280,32]{1,2,0:T(8,128)S(1)}, f32[2,1280,32]{1,2,0:T(8,128)}, u32[]{:S(2)}) copy-start(f32[2,1280,32]{1,2,0:T(8,128)} %convolution_add_fusion.7) | copy-start | bytes 983044 | tf_op jit(solution)/shard_map/while
  271.6 7.5 %copy-start = (f32[2,1280,32]{1,2,0:T(8,128)S(1)}, f32[2,1280,32]{1,2,0:T(8,128)}, u32[]{:S(2)}) copy-start(f32[2,1280,32]{1,2,0:T(8,128)} %convolution_add_fusion.7) | copy-start | bytes 983044 | tf_op jit(solution)/shard_map/while
  280.5 47.9 %copy-start.3 = (bf16[2,2,64,1280]{3,2,1,0:T(8,128)(2,1)S(1)}, bf16[2,2,64,1280]{3,2,1,0:T(8,128)(2,1)}, u32[]{:S(2)}) copy-start(bf16[2,2,64,1280]{3,2,1,0:T(8,128)(2,1)} %copy-done.2) | copy-start | bytes 1966084
  280.5 49.1 %copy-start.6 = (f32[2,2,1280,32]{2,3,1,0:T(8,128)S(1)}, f32[2,2,1280,32]{2,3,1,0:T(8,128)}, u32[]{:S(2)}) copy-start(f32[2,2,1280,32]{2,3,1,0:T(8,128)} %fusion.101) | copy-start | bytes 1966084
  280.5 49.1 %copy-start.7 = (bf16[2,2,64,1280]{3,2,1,0:T(8,128)(2,1)S(1)}, bf16[2,2,64,1280]{3,2,1,0:T(8,128)(2,1)}, u32[]{:S(2)}) copy-start(bf16[2,2,64,1280]{3,2,1,0:T(8,128)(2,1)} %param.7) | copy-start | bytes 1966084
Sparse Core Ops, SparseCore 0:
  67.9 132.0 all-reduce.4
where the time goes:
time: 340 us; the launch traced here: 338 us
  waiting for transfers between devices  124 us (36%)
  local copies, waits for them, and re-layouts  109 us (32%)
  blocking collectives  41.7 us (12%)
  matrix products  28.3 us (8%)
  between operations  14.4 us (4%)
  starting transfers between devices  13.8 us (4%)
  other arithmetic  6.97 us (2%)
    psum x1, waiting for transfers between devices, shards(): totals = lax.psum((spatial_grad, bias_grad, temporal_grad), ('gz', 'ta'))  124 us
    psum x1, blocking collectives, shards(): totals = lax.psum((spatial_grad, bias_grad, temporal_grad), ('gz', 'ta'))  41.7 us
    slice x4, local copies, waits for them, and re-layouts, adjoint_frame(): grad_columns[0:plane_count]  25.7 us
    reshape x1, local copies, waits for them, and re-layouts, unfold(): return stacked.reshape(leading[:-1] + (9 * leading[-1], ROWS * COLS))  15.8 us
    slice x2, local copies, waits for them, and re-layouts, adjoint_frame(): grad_columns[1:plane_count + 1]  14.8 us
    slice x2, local copies, waits for them, and re-layouts, adjoint_frame(): grad_columns[2:plane_count + 2]  14.8 us
    unnamed x33, local copies, waits for them, and re-layouts  12.3 us
    ppermute x4, starting transfers between devices, with_halo(): lax.ppermute(tail, axis, [(i, (i + 1) % count) for i in range(ends)])  8.3 us
  transfers between devices with their start and end apart: 9, of which 1 were waited for; matrix products, arithmetic and copies ran while one was open for 38% of the time, Pallas kernels for 0%

commit v1 on v0

--- a/solution.py
+++ b/solution.py
@@ -179,7 +179,7 @@
 
     input_grad = lax.map(adjoint_frame, grad_planes)
     grad_in = (grad_front.astype(jnp.float32) + input_grad).astype(jnp.bfloat16)
-    totals = lax.psum((spatial_grad, bias_grad, temporal_grad), ("gz", "ta"))
+    totals = lax.psum(lax.psum((spatial_grad, bias_grad, temporal_grad), "ta"), "gz")
     factor = 1.0 / math.sqrt(
         frame_count * lax.axis_size("ta") * plane_count * lax.axis_size("gz") * ROWS * COLS
     )

time: 340 us -> 271 us (0.80)
  waiting for transfers between devices: 124 us -> 29.1 us
  blocking collectives: 41.7 us -> 67.2 us
    psum x1 -> x2, waiting for transfers between devices: 124 us -> 29 us  [the longest x1 29 us: shards(): lax.psum((spatial_grad, bias_grad, temporal_grad), 'ta')]
    psum x1 -> x2, blocking collectives: 41.7 us -> 67.2 us  [the longest x1 59.6 us: shards(): lax.psum(lax.psum((spatial_grad, bias_grad, temporal_grad), 'ta'), 'gz')]
  transfers between devices with their start and end apart: 9 -> 10, of which waited for: 1 -> 1; matrix products, arithmetic and copies ran while one was open for 38% -> 50% of each run, Pallas kernels for 0% -> 0%
where the time goes in v1:
time: 271 us; the launch traced here: 269 us
  local copies, waits for them, and re-layouts  109 us (40%)
  blocking collectives  67.2 us (25%)
  waiting for transfers between devices  29.1 us (11%)
  matrix products  28.3 us (10%)
  between operations  14.4 us (5%)
  starting transfers between devices  13.8 us (5%)
  other arithmetic  7 us (3%)
    psum x1, blocking collectives, shards(): lax.psum(lax.psum((spatial_grad, bias_grad, temporal_grad), 'ta'), 'gz')  59.6 us
    psum x1, waiting for transfers between devices, shards(): lax.psum((spatial_grad, bias_grad, temporal_grad), 'ta')  29 us
    slice x4, local copies, waits for them, and re-layouts, adjoint_frame(): grad_columns[0:plane_count]  26 us
    reshape x1, local copies, waits for them, and re-layouts, unfold(): return stacked.reshape(leading[:-1] + (9 * leading[-1], ROWS * COLS))  15.8 us
    slice x2, local copies, waits for them, and re-layouts, adjoint_frame(): grad_columns[1:plane_count + 1]  14.9 us
    slice x2, local copies, waits for them, and re-layouts, adjoint_frame(): grad_columns[2:plane_count + 2]  14.8 us
    unnamed x33, local copies, waits for them, and re-layouts  12.3 us
    ppermute x4, starting transfers between devices, with_halo(): lax.ppermute(tail, axis, [(i, (i + 1) % count) for i in range(ends)])  8.27 us
  transfers between devices with their start and end apart: 10, of which 1 were waited for; matrix products, arithmetic and copies ran while one was open for 50% of the time, Pallas kernels for 0%

profile of v1, /device:TPU:0, one launch (start us, length us, event | category | flops | bytes accessed | tf_op | source)
XLA Modules:
  0.0 269.0 jit_solution(12618710953479311593)
XLA Ops:
  8.3 2.4 collective-permute-start
  13.7 2.3 collective-permute-start.4
  16.1 1.7 slice.236
  31.7 1.7 fusion.66
  36.2 15.8 %reshape.46 = bf16[2,4,288,1280]{3,2,1,0:T(8,128)(2,1)} reshape(bf16[2,4,9,32,8,160]{5,4,3,2,1,0:T(8,128)(2,1)} %fusion.70) | data formatting | bytes 11796480 | tf_op jit(solution)/shard_map/reshape | solution.py:38
  52.0 2.7 %fusion.40 = f32[2,2,1280,64]{2,3,1,0:T(8,128)S(1)} fusion(bf16[2,4,288,1280]{3,2,1,0:T(8,128)(2,1)} %reshape.46, bf16[3,64,288]{2,1,0:T(8,128)(2,1)S(1)} %copy-done.10), kind=kOutput, calls=%fused_computation.63 | convolution fusion | flops 188743680 | bytes 4308992 | tf_op jit(solution)/shard_map/oi,fzir->fzor/dot_general | solution.py:42
  54.8 2.6 convolution_add_fusion.4
  59.9 1.8 convert_reduce_fusion
  66.3 4.3 %collective-permute-start.6 = (bf16[2,1,64,1280]{3,2,1,0:T(8,128)(2,1)S(1)}, bf16[2,1,64,1280]{3,2,1,0:T(8,128)(2,1)S(1)}, u32[]{:S(2)}, u32[]{:S(2)}) collective-permute-start(bf16[2,1,64,1280]{3,2,1,0:T(8,128)(2,1)S(1)} %get-tuple-element.74), channel_id=1, source_target_pairs={{0,2},{2,4},{4,6},{6,8},{8,10},{10,12},{12,14},{14,16},{16,18},{18... | collective-permute-start | bytes 983048 | tf_op jit(solution)/shard_map/ppermute | solution.py:19
  75.9 29.0 %all-reduce.7.cloned.1.call-done = f32[3,64,288]{2,1,0:T(8,128)} async-done(((f32[3,64,288]{2,1,0:T(8,128)}), f32[3,64,288]{2,1,0:T(8,128)}) %all-reduce.7.cloned.1.call-update) | async-done | bytes 221200 | tf_op jit(solution)/shard_map/psum | solution.py:182
  106.1 77.8 %while.12 = (s32[]{:T(128)}, f32[2,2,32,1280]{3,2,1,0:T(8,128)}, bf16[2,4,64,1280]{3,2,1,0:T(8,128)(2,1)}, bf16[3,32,576]{2,1,0:T(8,128)(2,1)S(1)}, s32[]{:T(128)}) while((s32[]{:T(128)}, f32[2,2,32,1280]{3,2,1,0:T(8,128)}, bf16[2,4,64,1280]{3,2,1,0:T(8,128)(2,1)}, bf16[3,32,576]{2,1,0:T(8,128)(2,1)S(1)}, s32[]{:T(128)}) %tuple.40), condition=%wide.region_1.2_spmd, body=%wide.region_0.1_spmd.sunk | while | flops 283279360 | bytes 69722216 | solution.py:180
  113.9 5.5 %fusion.165 = (bf16[2,9,64,8,160]{4,3,2,1,0:T(8,128)(2,1)}, bf16[2,9,64,8,160]{4,3,2,1,0:T(8,128)(2,1)}, bf16[2,9,64,8,160]{4,3,2,1,0:T(8,128)(2,1)}) fusion(bf16[4,9,64,8,160]{4,3,2,1,0:T(8,128)(2,1)S(1)} %fusion.164), kind=kLoop, calls=%fused_computation.155.clone.1 | loop fusion | bytes 17694720 | tf_op jit(solution)/shard_map/while/body/eval_jaxpr/slice | solution.py:175
  119.4 7.4 %slice.457 = bf16[2,576,1280]{2,1,0:T(8,128)(2,1)S(1)} reshape(bf16[2,9,64,8,160]{4,3,2,1,0:T(8,128)(2,1)} %get-tuple-element.114) | data formatting | bytes 5898240 | tf_op jit(solution)/shard_map/while/body/eval_jaxpr/slice | solution.py:163
  127.4 7.4 %slice.458 = bf16[2,576,1280]{2,1,0:T(8,128)(2,1)S(1)} reshape(bf16[2,9,64,8,160]{4,3,2,1,0:T(8,128)(2,1)} %get-tuple-element.115) | data formatting | bytes 5898240 | tf_op jit(solution)/shard_map/while/body/eval_jaxpr/slice | solution.py:169
  136.2 7.5 %slice.459 = bf16[2,576,1280]{2,1,0:T(8,128)(2,1)S(1)} reshape(bf16[2,9,64,8,160]{4,3,2,1,0:T(8,128)(2,1)} %get-tuple-element.116) | data formatting | bytes 5898240 | tf_op jit(solution)/shard_map/while/body/eval_jaxpr/slice | solution.py:175
  152.8 5.5 %fusion.165 = (bf16[2,9,64,8,160]{4,3,2,1,0:T(8,128)(2,1)}, bf16[2,9,64,8,160]{4,3,2,1,0:T(8,128)(2,1)}, bf16[2,9,64,8,160]{4,3,2,1,0:T(8,128)(2,1)}) fusion(bf16[4,9,64,8,160]{4,3,2,1,0:T(8,128)(2,1)S(1)} %fusion.164), kind=kLoop, calls=%fused_computation.155.clone.1 | loop fusion | bytes 17694720 | tf_op jit(solution)/shard_map/while/body/eval_jaxpr/slice | solution.py:175
  158.3 7.4 %slice.457 = bf16[2,576,1280]{2,1,0:T(8,128)(2,1)S(1)} reshape(bf16[2,9,64,8,160]{4,3,2,1,0:T(8,128)(2,1)} %get-tuple-element.114) | data formatting | bytes 5898240 | tf_op jit(solution)/shard_map/while/body/eval_jaxpr/slice | solution.py:163
  166.3 7.4 %slice.458 = bf16[2,576,1280]{2,1,0:T(8,128)(2,1)S(1)} reshape(bf16[2,9,64,8,160]{4,3,2,1,0:T(8,128)(2,1)} %get-tuple-element.115) | data formatting | bytes 5898240 | tf_op jit(solution)/shard_map/while/body/eval_jaxpr/slice | solution.py:169
  175.1 7.5 %slice.459 = bf16[2,576,1280]{2,1,0:T(8,128)(2,1)S(1)} reshape(bf16[2,9,64,8,160]{4,3,2,1,0:T(8,128)(2,1)} %get-tuple-element.116) | data formatting | bytes 5898240 | tf_op jit(solution)/shard_map/while/body/eval_jaxpr/slice | solution.py:175
  183.9 2.1 add_convert_fusion
  189.0 7.5 %all-reduce.3 = (f32[64]{0:T(128)S(1)}, f32[3,32,64]{2,1,0:T(8,128)S(1)}) all-reduce(f32[64]{0:T(128)S(1)} %get-tuple-element.84, f32[3,32,64]{2,1,0:T(8,128)S(1)} %pad_maximum_fusion.3), channel_id=1, replica_groups=mesh['gz'=16,'ta'=2] {'ta'}, use_global_device_ids=true, to_apply=%region_5.6 | all-reduce | flops 6208 | bytes 49664 | tf_op jit(solution)/shard_map/psum | solution.py:182
  196.5 59.6 %all-reduce.2 = (f32[64]{0:T(128)S(1)}, f32[3,32,64]{2,1,0:T(8,128)S(1)}) all-reduce(f32[64]{0:T(128)S(1)} %get-tuple-element.69, f32[3,32,64]{2,1,0:T(8,128)S(1)} %get-tuple-element.70), channel_id=1, replica_groups=mesh['gz'=16,'ta'=2] {'gz'}, use_global_device_ids=true, to_apply=%region_6.7 | all-reduce | flops 6208 | bytes 49664 | tf_op jit(solution)/shard_map/psum | solution.py:182
  258.0 1.9 fusion.45
  260.5 1.7 broadcast_multiply_fusion
  (114 shorter events, 61.5 us)
Async XLA Ops:
  7.2 13.6 %slice-start = ((bf16[2,2,64,1280]{3,2,1,0:T(8,128)(2,1)}), bf16[2,2,32,1280]{3,2,1,0:T(8,128)(2,1)S(1)}, s32[]{:S(2)}) async-start(bf16[2,2,64,1280]{3,2,1,0:T(8,128)(2,1)} %param.7), calls=%async_computation.2 | async-start | bytes 655360 | tf_op jit(solution)/shard_map/slice | solution.py:93
  7.2 12.1 %copy-start.4 = (bf16[2,2,64,1280]{3,2,1,0:T(8,128)(2,1)S(1)}, bf16[2,2,64,1280]{3,2,1,0:T(8,128)(2,1)}, u32[]{:S(2)}) copy-start(bf16[2,2,64,1280]{3,2,1,0:T(8,128)(2,1)} %param.8) | copy-start | bytes 1966084
  7.2 12.1 %copy-start.11 = (bf16[3,32,64]{2,1,0:T(8,128)(2,1)S(1)}, bf16[3,32,64]{2,1,0:T(8,128)(2,1)}, u32[]{:S(2)}) copy-start(bf16[3,32,64]{2,1,0:T(8,128)(2,1)} %param.11) | copy-start | bytes 36868
  7.2 97.6 %all-reduce.7.cloned.1.call-start = ((), (), s32[]{:S(2)}) async-start(), calls=%async_computation | async-start | bytes 589824 | tf_op jit(solution)/shard_map/psum | solution.py:182
  8.3 12.4 %collective-permute-start = (bf16[2,1,32,1280]{3,2,1,0:T(8,128)(2,1)S(1)}, bf16[2,1,32,1280]{3,2,1,0:T(8,128)(2,1)S(1)}, u32[]{:S(2)}, u32[]{:S(2)}) collective-permute-start(bf16[2,1,32,1280]{3,2,1,0:T(8,128)(2,1)S(1)} %get-tuple-element.80), channel_id=1, source_target_pairs={{0,2},{2,4},{4,6},{6,8},{8,10},{10,12},{12,14},{14,16},{16,18},{18... | collective-permute-start | bytes 491528 | tf_op jit(solution)/shard_map/ppermute | solution.py:19
  10.8 10.0 %collective-permute-start.1 = (bf16[2,1,32,1280]{3,2,1,0:T(8,128)(2,1)S(1)}, bf16[2,1,32,1280]{3,2,1,0:T(8,128)(2,1)S(1)}, u32[]{:S(2)}, u32[]{:S(2)}) collective-permute-start(bf16[2,1,32,1280]{3,2,1,0:T(8,128)(2,1)S(1)} %get-tuple-element.81), channel_id=1, source_target_pairs={{2,0},{4,2},{6,4},{8,6},{10,8},{12,10},{14,12},{16,14},{18,16},{20... | collective-permute-start | bytes 491528 | tf_op jit(solution)/shard_map/ppermute | solution.py:21
  13.7 46.2 %collective-permute-start.4 = (bf16[1,2,32,1280]{3,2,1,0:T(8,128)(2,1)}, bf16[1,2,32,1280]{3,2,1,0:T(8,128)(2,1)}, u32[]{:S(2)}, u32[]{:S(2)}) collective-permute-start(bf16[1,2,32,1280]{3,2,1,0:T(8,128)(2,1)} %get-tuple-element.76), channel_id=1, source_target_pairs={{1,0},{0,1},{3,2},{2,3},{5,4},{4,5},{7,6},{6,7},{9,8},{8,9},{11,10... | collective-permute-start | bytes 491528 | tf_op jit(solution)/shard_map/ppermute | solution.py:21
  16.1 42.3 %collective-permute-start.5 = (bf16[1,2,32,1280]{3,2,1,0:T(8,128)(2,1)S(1)}, bf16[1,2,32,1280]{3,2,1,0:T(8,128)(2,1)}, u32[]{:S(2)}, u32[]{:S(2)}) collective-permute-start(bf16[1,2,32,1280]{3,2,1,0:T(8,128)(2,1)S(1)} %get-tuple-element.77), channel_id=1, source_target_pairs={{0,1},{1,0},{2,3},{3,2},{4,5},{5,4},{6,7},{7,6},{8,9},{9,8},{10,11... | collective-permute-start | bytes 491528 | tf_op jit(solution)/shard_map/ppermute | solution.py:19
  36.2 15.8 %copy-start.10 = (bf16[3,64,288]{2,1,0:T(8,128)(2,1)S(1)}, bf16[3,64,288]{2,1,0:T(8,128)(2,1)}, u32[]{:S(2)}) copy-start(bf16[3,64,288]{2,1,0:T(8,128)(2,1)} %param.9) | copy-start | bytes 331780
  52.0 5.4 %copy-start.1 = (bf16[2,4,288,1280]{3,2,1,0:T(8,128)(2,1)S(1)}, bf16[2,4,288,1280]{3,2,1,0:T(8,128)(2,1)}, u32[]{:S(2)}) copy-start(bf16[2,4,288,1280]{3,2,1,0:T(8,128)(2,1)} %reshape.46) | copy-start | bytes 17694724
  54.7 2.7 copy-start.12
  57.4 2.5 copy-start.9
  58.4 16.4 %copy-start.2 = (bf16[2,2,64,1280]{3,2,1,0:T(8,128)(2,1)}, bf16[2,2,64,1280]{3,2,1,0:T(8,128)(2,1)S(1)}, u32[]{:S(2)}) copy-start(bf16[2,2,64,1280]{3,2,1,0:T(8,128)(2,1)S(1)} %get-tuple-element.82) | copy-start | bytes 1966084
  63.9 1.2 copy-start.5
  66.3 38.6 %collective-permute-start.6 = (bf16[2,1,64,1280]{3,2,1,0:T(8,128)(2,1)S(1)}, bf16[2,1,64,1280]{3,2,1,0:T(8,128)(2,1)S(1)}, u32[]{:S(2)}, u32[]{:S(2)}) collective-permute-start(bf16[2,1,64,1280]{3,2,1,0:T(8,128)(2,1)S(1)} %get-tuple-element.74), channel_id=1, source_target_pairs={{0,2},{2,4},{4,6},{6,8},{8,10},{10,12},{12,14},{14,16},{16,18},{18... | collective-permute-start | bytes 983048 | tf_op jit(solution)/shard_map/ppermute | solution.py:19
  70.6 34.3 %collective-permute-start.7 = (bf16[2,1,64,1280]{3,2,1,0:T(8,128)(2,1)S(1)}, bf16[2,1,64,1280]{3,2,1,0:T(8,128)(2,1)S(1)}, u32[]{:S(2)}, u32[]{:S(2)}) collective-permute-start(bf16[2,1,64,1280]{3,2,1,0:T(8,128)(2,1)S(1)} %get-tuple-element.75), channel_id=1, source_target_pairs={{2,0},{4,2},{6,4},{8,6},{10,8},{12,10},{14,12},{16,14},{18,16},{20... | collective-permute-start | bytes 983048 | tf_op jit(solution)/shard_map/ppermute | solution.py:21
  72.6 187.8 %all-reduce.9.cloned.1.call-start = ((), (), s32[]{:S(2)}) async-start(), calls=%async_computation.1 | async-start | bytes 589824 | tf_op jit(solution)/shard_map/psum | solution.py:182
  72.7 113.4 %collective-permute-start.2 = (bf16[1,2,64,1280]{3,2,1,0:T(8,128)(2,1)}, bf16[1,2,64,1280]{3,2,1,0:T(8,128)(2,1)}, u32[]{:S(2)}, u32[]{:S(2)}) collective-permute-start(bf16[1,2,64,1280]{3,2,1,0:T(8,128)(2,1)} %get-tuple-element.78), channel_id=1, source_target_pairs={{0,1},{1,0},{2,3},{3,2},{4,5},{5,4},{6,7},{7,6},{8,9},{9,8},{10,11... | collective-permute-start | bytes 983048 | tf_op jit(solution)/shard_map/ppermute | solution.py:19
  74.2 113.3 %collective-permute-start.3 = (bf16[1,2,64,1280]{3,2,1,0:T(8,128)(2,1)}, bf16[1,2,64,1280]{3,2,1,0:T(8,128)(2,1)}, u32[]{:S(2)}, u32[]{:S(2)}) collective-permute-start(bf16[1,2,64,1280]{3,2,1,0:T(8,128)(2,1)} %get-tuple-element.79), channel_id=1, source_target_pairs={{1,0},{0,1},{3,2},{2,3},{5,4},{4,5},{7,6},{6,7},{9,8},{8,9},{11,10... | collective-permute-start | bytes 983048 | tf_op jit(solution)/shard_map/ppermute | solution.py:21
  136.2 7.5 %copy-start = (f32[2,1280,32]{1,2,0:T(8,128)S(1)}, f32[2,1280,32]{1,2,0:T(8,128)}, u32[]{:S(2)}) copy-start(f32[2,1280,32]{1,2,0:T(8,128)} %convolution_add_fusion.7) | copy-start | bytes 983044 | tf_op jit(solution)/shard_map/while
  175.1 7.5 %copy-start = (f32[2,1280,32]{1,2,0:T(8,128)S(1)}, f32[2,1280,32]{1,2,0:T(8,128)}, u32[]{:S(2)}) copy-start(f32[2,1280,32]{1,2,0:T(8,128)} %convolution_add_fusion.7) | copy-start | bytes 983044 | tf_op jit(solution)/shard_map/while
  183.9 72.9 %copy-start.3 = (bf16[2,2,64,1280]{3,2,1,0:T(8,128)(2,1)S(1)}, bf16[2,2,64,1280]{3,2,1,0:T(8,128)(2,1)}, u32[]{:S(2)}) copy-start(bf16[2,2,64,1280]{3,2,1,0:T(8,128)(2,1)} %copy-done.2) | copy-start | bytes 1966084
  183.9 74.1 %copy-start.6 = (f32[2,2,1280,32]{2,3,1,0:T(8,128)S(1)}, f32[2,2,1280,32]{2,3,1,0:T(8,128)}, u32[]{:S(2)}) copy-start(f32[2,2,1280,32]{2,3,1,0:T(8,128)} %fusion.101) | copy-start | bytes 1966084
  183.9 74.1 %copy-start.7 = (bf16[2,2,64,1280]{3,2,1,0:T(8,128)(2,1)S(1)}, bf16[2,2,64,1280]{3,2,1,0:T(8,128)(2,1)}, u32[]{:S(2)}) copy-start(bf16[2,2,64,1280]{3,2,1,0:T(8,128)(2,1)} %param.7) | copy-start | bytes 1966084
  (1 other events, 1.0 us)
Sparse Core Ops, SparseCore 0:
  72.7 32.0 all-reduce.6
  108.2 91.1 all-reduce.8
